TPU v7x, 128 devices: a whole 4x4x4 slice. The times are simulated.
128 devices in a mesh: rep: 4 (over z_lo, core), shard: 32 (over z_hi, x, y).
Axes of the slice: x: 4, y: 4, z: 4 (z_hi: 2, z_lo: 2; z = z_hi * 2 + z_lo), core: 2. Of those that a mesh axis runs over, the one named last changes fastest.
Arguments:
- local_layers: float32 [4, 4, 768, 768], P('rep', None, 'shard'), may hold values from -6 to 6
- global_layers: float32 [4, 768, 768], P(None, 'shard'), may hold values from -6 to 6
- momentum_layers: float32 [4, 768, 768], P(None, 'shard'), may hold values from -3 to 3
- local_embed: float32 [4, 32128, 768], P('rep', 'shard'), may hold values from -6 to 6
- global_embed: float32 [32128, 768], P('shard'), may hold values from -6 to 6
- momentum_embed: float32 [32128, 768], P('shard'), may hold values from -3 to 3
- proj_basis: float32 [768, 64], replicated, may hold values from -0.21875 to 0.21875
Outputs:
- mean_layers: float32 [4, 768, 768], P(None, 'shard')
- moment_layers: float32 [4, 768, 768], P(None, 'shard')
- weights_layers: float32 [4, 768, 768], P(None, 'shard')
- copy_layers: bfloat16 [4, 768, 768], replicated
- mean_embed: float32 [32128, 768], P('shard')
- moment_embed: float32 [32128, 768], P('shard')
- weights_embed: float32 [32128, 768], P('shard')
All inputs are finite; a program needn't handle non-finite values.
Results may differ from a plain program's by a relative error of at most 0.0085.
Values may be sent and summed in bfloat16 or wider, within the bound.
A program may use at most 128 MiB of HBM per device.

v0:
```python
import jax
import jax.numpy as jnp
from jax import lax
from jax.sharding import PartitionSpec as P

OUTER_MOMENTUM = 0.9
OUTER_RATE = 0.7


def outer_update(mean_diff, momentum, weights):
    new_moment = OUTER_MOMENTUM * momentum + mean_diff
    new_weights = weights - OUTER_RATE * (mean_diff + OUTER_MOMENTUM * new_moment)
    return (new_moment, new_weights)


def body(
    local_layers,
    global_layers,
    momentum_layers,
    local_embed,
    global_embed,
    momentum_embed,
    proj_basis,
):
    groups = lax.axis_size("rep")
    layer_diff = global_layers - local_layers[0]
    mean_layers = lax.psum(layer_diff, "rep") / groups
    moment_layers, weights_layers = outer_update(mean_layers, momentum_layers, global_layers)
    copy_layers = lax.all_gather(weights_layers.astype(jnp.bfloat16), "shard", axis=1, tiled=True)
    embed_diff = global_embed - local_embed[0]
    embed_full = lax.psum(embed_diff.astype(jnp.bfloat16), "rep").astype(jnp.float32) / groups
    low_mean = jnp.dot(embed_full, proj_basis, precision=lax.Precision.HIGHEST)
    mean_embed = jnp.dot(low_mean, proj_basis.T, precision=lax.Precision.HIGHEST)
    moment_embed, weights_embed = outer_update(mean_embed, momentum_embed, global_embed)
    return (
        mean_layers,
        moment_layers,
        weights_layers,
        copy_layers,
        mean_embed,
        moment_embed,
        weights_embed,
    )


def solution(mesh):
    in_specs = (
        P("rep", None, "shard", None),
        P(None, "shard", None),
        P(None, "shard", None),
        P("rep", "shard", None),
        P("shard", None),
        P("shard", None),
        P(),
    )
    out_specs = (
        P(None, "shard", None),
        P(None, "shard", None),
        P(None, "shard", None),
        P(),
        P("shard", None),
        P("shard", None),
        P("shard", None),
    )
    return jax.shard_map(body, mesh=mesh, in_specs=in_specs, out_specs=out_specs, check_vma=False)
```

profile of v0, /device:TPU:1, one launch (start us, length us, event | category | flops | bytes accessed | tf_op | source)
XLA Modules:
  0.0 203.3 jit_solution(15389995576287154729)
XLA Ops:
  7.2 0.0 copy-start
  7.2 0.0 all-reduce.3.cloned.1.call-start
  7.2 1.8 bitcast_subtract_fusion.1
  9.1 0.0 all-reduce.3.cloned.1.call-update
  9.1 0.0 all-reduce.5.cloned.1.call-start
  9.1 4.3 %fusion = bf16[1004,768]{1,0:T(8,128)(2,1)} fusion(f32[1004,768]{1,0:T(8,128)} %param.11, f32[1,1004,768]{2,0,1:T(1,128)} %param.10), kind=kLoop, calls=%fused_computation.1 | loop fusion | flops 1542144 | bytes 7710720 | tf_op jit(solution)/shard_map/convert_element_type | solution.py:31
  13.5 0.0 copy-start.1
  13.5 0.0 all-reduce.5.cloned.1.call-update
  13.5 0.0 all-gather.2.cloned.1.call-start
  13.5 37.9 %all-reduce.3.cloned.1.call-done = f32[4,24,768]{2,1,0:T(8,128)} async-done(((f32[4,24,768]{2,1,0:T(8,128)}), f32[4,24,768]{2,1,0:T(8,128)}) %all-reduce.3.cloned.1.call-update) | async-done | bytes 294928 | tf_op jit(solution)/shard_map/psum | solution.py:27
  51.4 2.2 %fusion.6 = (bf16[4,24,768]{2,1,0:T(8,128)(2,1)}, f32[4,24,768]{2,1,0:T(8,128)}, f32[4,24,768]{2,1,0:T(8,128)}, f32[4,24,768]{2,1,0:T(8,128)}) fusion(f32[4,24,768]{2,1,0:T(8,128)} %param.8, f32[4,24,768]{2,1,0:T(8,128)} %param.9, f32[4,24,768]{2,1,0:T(8,128)} %all-reduce.3.cloned.1.call-done), kind=kLoop, calls=%fused_computation.13 | loop fusion | flops 589824 | bytes 1916928 | tf_op jit(solution)/shard_map/convert_element_type | solution.py:29
  53.6 0.0 all-gather.2.cloned.1.call-update
  53.6 50.5 %all-reduce.5.cloned.1.call-done = bf16[1004,768]{1,0:T(8,128)(2,1)} async-done(((bf16[1004,768]{1,0:T(8,128)(2,1)}), bf16[1004,768]{1,0:T(8,128)(2,1)}) %all-reduce.5.cloned.1.call-update) | async-done | bytes 1542160 | tf_op jit(solution)/shard_map/psum | solution.py:31
  104.1 0.0 copy-done
  104.1 3.9 %fusion.1 = f32[1004,64]{1,0:T(8,128)S(1)} fusion(f32[768,64]{0,1:T(8,128)S(1)} %copy-done, bf16[1004,768]{1,0:T(8,128)(2,1)} %all-reduce.5.cloned.1.call-done), kind=kOutput, calls=%fused_computation.4 | convolution fusion | flops 593725440 | bytes 1995776 | tf_op jit(solution)/shard_map/dot_general | solution.py:32
  108.1 0.0 copy-done.1
  108.1 8.7 %multiply_subtract_fusion = (f32[1004,768]{1,0:T(8,128)}, f32[1004,768]{1,0:T(8,128)}, f32[1004,768]{1,0:T(8,128)}) fusion(f32[1004,768]{1,0:T(8,128)S(1)} %copy-done.1, f32[1004,768]{1,0:T(8,128)} %param.12, f32[1004,64]{1,0:T(8,128)S(1)} %fusion.1, f32[768,64]{0,1:T(8,128)S(1)} %copy-done), kind=kOutput, calls=%fused_computation.2 | convolution fusion | flops 596809728 | bytes 15875072 | tf_op jit(solution)/shard_map/dot_general | solution.py:33
  116.7 75.2 %all-gather.2.cloned.1.call-done = bf16[4,768,768]{2,1,0:T(8,128)(2,1)} async-done(((bf16[4,24,768]{2,1,0:T(8,128)(2,1)}), bf16[4,768,768]{2,1,0:T(8,128)(2,1)}) %all-gather.2.cloned.1.call-update) | async-done | bytes 4718608 | tf_op jit(solution)/shard_map/all_gather | solution.py:29
  191.9 4.8 %copy.19 = bf16[4,768,768]{2,1,0:T(8,128)(2,1)} copy(bf16[4,768,768]{2,1,0:T(8,128)(2,1)} %all-gather.2.cloned.1.call-done) | data formatting | bytes 9437184
Async XLA Ops:
  7.2 96.9 %copy-start = (f32[768,64]{0,1:T(8,128)S(1)}, f32[768,64]{0,1:T(8,128)}, u32[]{:S(2)}) copy-start(f32[768,64]{0,1:T(8,128)} %param.13) | copy-start | bytes 589828
  7.2 44.2 %all-reduce.3.cloned.1.call-start = ((), (), s32[]{:S(2)}) async-start(), calls=%async_computation | async-start | bytes 589824 | tf_op jit(solution)/shard_map/psum | solution.py:27
  9.1 95.0 %all-reduce.5.cloned.1.call-start = ((), (), s32[]{:S(2)}) async-start(), calls=%async_computation.2 | async-start | bytes 3096576 | tf_op jit(solution)/shard_map/psum | solution.py:31
  13.5 94.6 %copy-start.1 = (f32[1004,768]{1,0:T(8,128)S(1)}, f32[1004,768]{1,0:T(8,128)}, u32[]{:S(2)}) copy-start(f32[1004,768]{1,0:T(8,128)} %param.11) | copy-start | bytes 9252868
  13.5 178.4 %all-gather.2.cloned.1.call-start = ((), (), s32[]{:S(2)}) async-start(), calls=%async_computation.1 | async-start | bytes 4866048 | tf_op jit(solution)/shard_map/all_gather | solution.py:29
Sparse Core Ops, SparseCore 0:
  11.1 40.2 all-reduce.2
  54.5 49.5 all-reduce.4
  107.8 84.1 all-gather.1
where the time goes:
time: 204 us; the launch traced here: 203 us
  waiting for transfers between devices  164 us (80%)
  between operations  13.8 us (7%)
  matrix products  12.6 us (6%)
  other arithmetic  8.33 us (4%)
  local copies, waits for them, and re-layouts  4.84 us (2%)
    all_gather x1, waiting for transfers between devices, body(): lax.all_gather(weights_layers.astype(jnp.bfloat16), 'shard', axis=1, tile...  75.2 us
    psum x1, waiting for transfers between devices, body(): lax.psum(embed_diff.astype(jnp.bfloat16), 'rep').astype(jnp.float32)  50.5 us
    psum x1, waiting for transfers between devices, body(): mean_layers = lax.psum(layer_diff, 'rep') / groups  37.9 us
    dot_general x1, matrix products, body(): jnp.dot(low_mean, proj_basis.T, precision=lax.Precision.HIGHEST)  8.65 us
    unnamed x5, local copies, waits for them, and re-layouts  4.84 us
    convert_element_type x1, other arithmetic, body(): embed_diff.astype(jnp.bfloat16)  4.34 us
  transfers between devices with their start and end apart: 3, of which 3 were waited for; matrix products, arithmetic and copies ran while one was open for 9% of the time, Pallas kernels for 0%

commit v1 on v0

v1 whole, which is shorter than its diff:
```python
import functools

import jax
import jax.numpy as jnp
from jax import lax
from jax.experimental import pallas as pl
from jax.experimental.pallas import tpu as pltpu
from jax.sharding import PartitionSpec as P

OUTER_MOMENTUM = 0.9
OUTER_RATE = 0.7
MESH = pl.DeviceIdType.MESH
HBM = pl.BlockSpec(memory_space=pl.ANY)
VMEM = pl.BlockSpec(memory_space=pltpu.VMEM)
X, Y, Z = 0, 1, 2
ORDERS = ((X, Y, Z), (Y, Z, X), (Z, X, Y))
DELTAS = (1, 3, 2)
HALF = 512


def outer_update(mean_diff, momentum, weights):
    new_moment = OUTER_MOMENTUM * momentum + mean_diff
    new_weights = weights - OUTER_RATE * (mean_diff + OUTER_MOMENTUM * new_moment)
    return (new_moment, new_weights)


def where_am_i():
    rep, shard = lax.axis_index("rep"), lax.axis_index("shard")
    z_low, core = lax.div(rep, 2), lax.rem(rep, 2)
    z_high, x, y = lax.div(shard, 16), lax.rem(lax.div(shard, 4), 4), lax.rem(shard, 4)
    return [x, y, z_high * 2 + z_low], core


def device(at, core):
    x, y, z = at
    return (lax.rem(z, 2) * 2 + core, lax.div(z, 2) * 16 + x * 4 + y)


def moved(at, axis, step):
    return [lax.rem(c + step, 4) if i == axis else c for i, c in enumerate(at)]


def piece(gathered, at, core, part):
    x, y, z = (slice(None) if c is None else c for c in at)
    z_low, z_high = (z, z) if isinstance(z, slice) else (lax.rem(z, 2), lax.div(z, 2))
    return gathered.at[z_low, core, z_high, x, y, part]


def exchange_kernel(
    ll, gl, ml, le, ge, me, bt,
    gathered, ge_v, me_v, low_total, layer_total,
    ll_v, gl_v, ml_v, ll_other, part_sum, part_other, le_v, bt_v, low, low_in, low_half, low_other,
    load_sem, rep_send, rep_recv, ring_send, ring_recv, pair_send, pair_recv,
):
    at, core = where_am_i()
    other = 1 - core
    z_low = lax.rem(at[Z], 2)
    twin_at = [at[X], at[Y], at[Z] + 1 - 2 * z_low]
    pair, twin = device(at, other), device(twin_at, core)
    rows = le.shape[0]

    def remote(src, dst, sems, i, to):
        send, recv = sems
        return pltpu.make_async_remote_copy(src, dst, send.at[i], recv.at[i], device_id=to, device_id_type=MESH)

    loads = [
        pltpu.make_async_copy(ll.at[:, core], ll_v, load_sem.at[0]),
        pltpu.make_async_copy(gl.at[:, core], gl_v, load_sem.at[1]),
        pltpu.make_async_copy(ml.at[z_low, core], ml_v, load_sem.at[2]),
        pltpu.make_async_copy(bt, bt_v, load_sem.at[3]),
        pltpu.make_async_copy(le, le_v, load_sem.at[4]),
        pltpu.make_async_copy(ge, ge_v, load_sem.at[5]),
        pltpu.make_async_copy(me, me_v, load_sem.at[6]),
    ]
    for load in loads:
        load.start()

    barrier = pltpu.get_barrier_semaphore()
    peers = [pair] + [device(moved(at, axis, step), core) for axis in (X, Y, Z) for step in DELTAS]
    for peer in peers:
        pl.semaphore_signal(barrier, inc=1, device_id=peer, device_id_type=MESH)
    pl.semaphore_wait(barrier, len(peers))

    rep = (rep_send, rep_recv)
    to_pair = remote(ll.at[:, other], ll_other, rep, 0, pair)
    to_pair.start()
    loads[0].wait()
    loads[1].wait()
    to_pair.wait_recv()
    part_sum[...] = (gl_v[...] - ll_v[...]) + (gl_v[...] - ll_other[...])
    first = remote(part_sum.at[1 - z_low], part_other.at[1 - z_low], rep, 1, twin)
    second = remote(part_sum.at[z_low], part_other.at[z_low], rep, 2, twin)
    first.start()
    second.start()

    loads[3].wait()
    loads[4].wait()
    loads[5].wait()
    basis = bt_v[...].astype(jnp.bfloat16)
    none = jnp.zeros_like(basis)
    left, right = jnp.concatenate([basis, none], 0), jnp.concatenate([none, basis], 0)
    nt = (((1,), (1,)), ((), ()))
    for start in range(0, HALF, 128):
        tail = min(128, rows - HALF - start)
        a, b = pl.ds(start, 128), pl.ds(HALF + start, tail)
        da = (ge_v[a, :] - le_v[a, :]).astype(jnp.bfloat16)
        db = (ge_v[b, :] - le_v[b, :]).astype(jnp.bfloat16)
        pa = lax.dot_general(da, left, nt, preferred_element_type=jnp.float32)
        pb = lax.dot_general(db, right, nt, preferred_element_type=jnp.float32)
        low[a, :] = pa
        low[pl.ds(start, tail), :] = low[pl.ds(start, tail), :] + pb
    quarter = HALF // 2
    mine, theirs = pl.ds(core * quarter, quarter), pl.ds(other * quarter, quarter)
    low_to_pair = remote(low.at[theirs], low_in, rep, 3, pair)
    low_to_pair.start()

    loads[2].wait()
    first_in = remote(part_sum.at[z_low], part_other.at[z_low], rep, 1, twin)
    first_in.wait_recv()
    mean = (part_sum[z_low] + part_other[z_low]) / 4
    _, weights = outer_update(mean, ml_v[...], gl_v[z_low])
    gathered[z_low, core, lax.div(at[Z], 2), at[X], at[Y]] = weights.astype(jnp.bfloat16).reshape(3, 8, 768)

    ring, pairs = (ring_send, ring_recv), (pair_send, pair_recv)
    started, expected = [], []

    def send(where, part, slot, to):
        copy = remote(piece(gathered, where, core, part), piece(gathered, where, core, part), ring, part * 18 + slot, to)
        copy.start()
        started.append(copy)

    def arrive(where, part, slot):
        ref = piece(gathered, where, core, part)
        remote(ref, ref, ring, part * 18 + slot, pair).wait_recv()
        share(where, part, slot)

    def share(where, part, slot):
        ref = piece(gathered, where, core, part)
        copy = remote(ref, ref, pairs, part * 19 + slot, pair)
        copy.start()
        started.append(copy)
        back = piece(gathered, where, other, part)
        expected.append(remote(back, back, pairs, part * 19 + slot, pair))

    def opened(where, *axes):
        return [None if i in axes else c for i, c in enumerate(where)]

    for part, (d1, d2, d3) in enumerate(ORDERS):
        for i, step in enumerate(DELTAS):
            send(at, part, i, device(moved(at, d1, step), core))
    for part in range(3):
        share(at, part, 18)

    low_to_pair.wait_recv()
    half = low[mine, :] + low_in[...]
    low_half[...] = half.astype(jnp.bfloat16)
    low_to_twin = remote(low_half, low_other, rep, 4, twin)
    low_to_twin.start()

    for part, (d1, d2, d3) in enumerate(ORDERS):
        for i, step in enumerate(DELTAS):
            arrive(moved(at, d1, 4 - step), part, i)
        row = opened(at, d1)
        for i, step in enumerate(DELTAS):
            send(row, part, 3 + i, device(moved(at, d2, step), core))
        for i, step in enumerate((1, 3)):
            send(row, part, 6 + i, device(moved(at, d3, step), core))

    low_to_twin.wait_recv()
    low_total[mine, :] = low_half[...].astype(jnp.float32) + low_other[...].astype(jnp.float32)
    low_back = remote(low_total.at[mine], low_total.at[mine], rep, 5, pair)
    low_back.start()

    second_in = remote(part_sum.at[1 - z_low], part_other.at[1 - z_low], rep, 2, twin)
    second_in.wait_recv()
    layer_total[:, core] = part_sum[...] + part_other[...]
    total_back = remote(layer_total.at[:, core], layer_total.at[:, core], rep, 6, pair)
    total_back.start()

    for j, back in enumerate(DELTAS):
        for part, (d1, d2, d3) in enumerate(ORDERS):
            row = opened(moved(at, d2, 4 - back), d1)
            arrive(row, part, 3 + j)
            for i, step in enumerate((1, 3)):
                send(row, part, 8 + 2 * j + i, device(moved(at, d3, step), core))

    for j, back in enumerate((0,) + DELTAS):
        for part, (d1, d2, d3) in enumerate(ORDERS):
            for i, step in enumerate((1, 3)):
                row = opened(moved(moved(at, d2, 4 - back), d3, 4 - step), d1)
                arrive(row, part, 6 + 2 * j + i)
                if j // 2 == i:
                    send(row, part, 14 + j, device(moved(at, d3, step), core))
    for j, back in enumerate((0,) + DELTAS):
        for part, (d1, d2, d3) in enumerate(ORDERS):
            arrive(opened(moved(moved(at, d2, 4 - back), d3, 2), d1), part, 14 + j)

    remote(low_total.at[theirs], low_total.at[theirs], rep, 5, pair).wait_recv()
    remote(layer_total.at[:, other], layer_total.at[:, other], rep, 6, pair).wait_recv()
    for copy in expected:
        copy.wait_recv()
    for copy in started + [to_pair, first, second, low_to_pair, low_to_twin, low_back, total_back]:
        copy.wait_send()
    loads[6].wait()


def finish_kernel(
    gathered, ge_v, me_v, low_total, layer_total, bt_v, gl_v, ml_v,
    mean_l, moment_l, weights_l, copy_l, mean_e, moment_e, weights_e,
    mean_lv, moment_lv, weights_lv, mean_v, moment_v, weights_v, sem, sem_e,
):
    rows = ge_v.shape[0]
    copies = []

    def put(src, dst, s):
        copy = pltpu.make_async_copy(src, dst, s)
        copy.start()
        copies.append(copy)

    put(gathered, copy_l, sem.at[0])
    basis = bt_v[...]
    high = basis.astype(jnp.bfloat16)
    none = jnp.zeros_like(high)
    left = jnp.concatenate([high, none, high, none], 0)
    right = jnp.concatenate([none, high, none, high], 0)
    for n, start in enumerate(range(0, rows, 128)):
        size = min(128, rows - start)
        packed = low_total[pl.ds(start % HALF, size), :] / 4
        top = packed.astype(jnp.bfloat16)
        rest = (packed - top.astype(jnp.float32)).astype(jnp.bfloat16)
        at = pl.ds(start, size)
        mean = jnp.dot(
            jnp.concatenate([top, rest], 1), left if start < HALF else right, preferred_element_type=jnp.float32
        )
        moment, weights = outer_update(mean, me_v[at, :], ge_v[at, :])
        for k, (value, buf, out) in enumerate(
            ((mean, mean_v, mean_e), (moment, moment_v, moment_e), (weights, weights_v, weights_e))
        ):
            buf[at, :] = value
            put(buf.at[at], out.at[at], sem_e.at[3 * n + k])
    mean = layer_total[...] / 4
    moment, weights = outer_update(mean, ml_v[...], gl_v[...])
    for k, (value, buf, out) in enumerate(
        ((mean, mean_lv, mean_l), (moment, moment_lv, moment_l), (weights, weights_lv, weights_l))
    ):
        buf[...] = value
        put(buf, out, sem.at[1 + k])
    for copy in copies:
        copy.wait()


def body(local_layers, global_layers, momentum_layers, local_embed, global_embed, momentum_embed, proj_basis):
    rows = global_embed.shape[0]
    grouped = (2, 2, 24, 768)
    ll, gl, ml = (a.reshape(grouped) for a in (local_layers, global_layers, momentum_layers))
    bt = proj_basis.T
    f32, bf16 = jnp.float32, jnp.bfloat16
    dma = pltpu.SemaphoreType.DMA
    gathered, ge_v, me_v, low_total, layer_total = pl.pallas_call(
        exchange_kernel,
        out_shape=(
            pltpu.VMEM((2, 2, 2, 4, 4, 3, 8, 768), bf16),
            pltpu.VMEM((rows, 768), f32),
            pltpu.VMEM((rows, 768), f32),
            pltpu.VMEM((HALF, 128), f32),
            pltpu.VMEM(grouped, f32),
        ),
        in_specs=[HBM] * 7,
        out_specs=(VMEM,) * 5,
        scratch_shapes=[
            pltpu.VMEM((2, 24, 768), f32),
            pltpu.VMEM((2, 24, 768), f32),
            pltpu.VMEM((24, 768), f32),
            pltpu.VMEM((2, 24, 768), f32),
            pltpu.VMEM((2, 24, 768), f32),
            pltpu.VMEM((2, 24, 768), f32),
            pltpu.VMEM((rows, 768), f32),
            pltpu.VMEM((64, 768), f32),
            pltpu.VMEM((HALF, 128), f32),
            pltpu.VMEM((HALF // 2, 128), f32),
            pltpu.VMEM((HALF // 2, 128), bf16),
            pltpu.VMEM((HALF // 2, 128), bf16),
            dma((7,)),
            dma((7,)),
            dma((7,)),
            dma((54,)),
            dma((54,)),
            dma((57,)),
            dma((57,)),
        ],
        compiler_params=pltpu.CompilerParams(
            collective_id=0, has_side_effects=True, vmem_limit_bytes=24 << 20
        ),
        name="exchange",
    )(ll, gl, ml, local_embed.reshape(rows, 768), global_embed, momentum_embed, bt)
    outs = pl.pallas_call(
        finish_kernel,
        out_shape=(
            *[jax.ShapeDtypeStruct(grouped, f32)] * 3,
            jax.ShapeDtypeStruct((2, 2, 2, 4, 4, 3, 8, 768), bf16),
            *[jax.ShapeDtypeStruct((rows, 768), f32)] * 3,
        ),
        in_specs=[VMEM] * 8,
        out_specs=(HBM,) * 7,
        scratch_shapes=[pltpu.VMEM(grouped, f32)] * 3 + [pltpu.VMEM((rows, 768), f32)] * 3 + [dma((4,)), dma((24,))],
        compiler_params=pltpu.CompilerParams(vmem_limit_bytes=24 << 20),
        name="finish",
    )(gathered, ge_v, me_v, low_total, layer_total, bt, gl, ml)
    layers = [a.reshape(4, 24, 768) for a in outs[:3]]
    return (*layers, outs[3].reshape(4, 768, 768), *outs[4:])


def solution(mesh):
    in_specs = (
        P("rep", None, "shard", None),
        P(None, "shard", None),
        P(None, "shard", None),
        P("rep", "shard", None),
        P("shard", None),
        P("shard", None),
        P(),
    )
    out_specs = (
        P(None, "shard", None),
        P(None, "shard", None),
        P(None, "shard", None),
        P(),
        P("shard", None),
        P("shard", None),
        P("shard", None),
    )
    return jax.shard_map(body, mesh=mesh, in_specs=in_specs, out_specs=out_specs, check_vma=False)
```

time: 204 us -> 46.7 us (0.23)
  waiting for transfers between devices: 164 us -> 0 us
  Pallas kernels: 0 us -> 40.9 us
  between operations: 13.8 us -> 0.7 us
  matrix products: 12.6 us -> 0 us
  other arithmetic: 8.33 us -> 0 us
    psum x2 -> x0, waiting for transfers between devices: 88.4 us -> none  [the longest x1 50.5 us: body(): lax.psum(embed_diff.astype(jnp.bfloat16), 'rep').astype(jnp.float32)]
    all_gather x1 -> x0, waiting for transfers between devices: 75.2 us -> none  [body(): lax.all_gather(weights_layers.astype(jnp.bfloat16), 'shard', axis=1, tile...]
    pallas_call x0 -> x2, Pallas kernels: none -> 40.9 us  [the longest x1 35.2 us: body(): pl.pallas_call(exchange_kernel, out_shape=(pltpu.VMEM((2, 2, 2, 4, 4, 3,...]
    dot_general x2 -> x0, matrix products: 12.6 us -> none  [the longest x1 8.65 us: body(): jnp.dot(low_mean, proj_basis.T, precision=lax.Precision.HIGHEST)]
    convert_element_type x2 -> x0, other arithmetic: 6.5 us -> none  [the longest x1 4.34 us: body(): embed_diff.astype(jnp.bfloat16)]
    unnamed x5 -> x13, local copies, waits for them, and re-layouts: 4.84 us -> 4.93 us
  transfers between devices with their start and end apart: 3 -> 0, of which waited for: 3 -> 0; matrix products, arithmetic and copies ran while one was open for 9% -> 0% of each run, Pallas kernels for 0% -> 0%
where the time goes in v1:
time: 46.7 us; the launch traced here: 46.6 us
  Pallas kernels  40.9 us (88%)
  local copies, waits for them, and re-layouts  4.93 us (11%)
  between operations  0.7 us (1%)
    pallas_call x1, Pallas kernels, body(): pl.pallas_call(exchange_kernel, out_shape=(pltpu.VMEM((2, 2, 2, 4, 4, 3,...  35.2 us
    pallas_call x1, Pallas kernels, body(): pl.pallas_call(finish_kernel, out_shape=(*[jax.ShapeDtypeStruct(grouped,...  5.74 us
    unnamed x13, local copies, waits for them, and re-layouts  4.93 us

profile of v1, /device:TPU:1, one launch (start us, length us, event | category | flops | bytes accessed | tf_op | source)
XLA Modules:
  0.0 46.6 jit_solution(10490278361377551129)
XLA Ops:
  0.6 0.0 copy-start.4
  0.6 0.0 copy-start
  0.7 0.0 copy-start.3
  0.7 0.0 copy-start.2
  0.7 0.0 copy-start.5
  0.7 2.2 %copy.16 = f32[1,1004,768]{2,1,0:T(8,128)S(1)} copy(f32[1,1004,768]{2,0,1:T(1,128)} %param.10) | data formatting | bytes 6168576
  2.9 0.0 copy-done.4
  2.9 0.6 %copy-done = f32[1004,768]{1,0:T(8,128)S(1)} copy-done((f32[1004,768]{1,0:T(8,128)S(1)}, f32[1004,768]{1,0:T(8,128)}, u32[]{:S(2)}) %copy-start) | copy-done | bytes 3084312
  3.6 0.0 copy-done.3
  3.6 0.1 copy-done.2
  3.7 0.1 copy-done.5
  3.7 0.0 copy-start.1
  3.7 1.9 %copy-done.1 = f32[1004,768]{1,0:T(8,128)S(1)} copy-done((f32[1004,768]{1,0:T(8,128)S(1)}, f32[1004,768]{1,0:T(8,128)}, u32[]{:S(2)}) %copy-start.1) | copy-done | bytes 3084312
  5.6 35.2 %exchange.1 = (bf16[2,2,2,4,4,3,8,768]{7,6,5,4,3,2,1,0:T(8,128)(2,1)S(1)}, f32[1004,768]{1,0:T(8,128)S(1)}, f32[1004,768]{1,0:T(8,128)S(1)}, f32[512,128]{1,0:T(8,128)S(1)}, f32[2,2,24,768]{3,2,1,0:T(8,128)S(1)}) custom-call(f32[2,2,24,768]{3,2,1,0:T(8,128)S(1)} %bitcast.18, f32[2,2,24,768]{3,2,1,0:T(8,128)S(1)} %bitcast.12, f32[2,2,24,768]{3,2,1,0:T(8,128)S(1)} %bitcast.14, ...), custom_call_target="tpu_custom_call" | custom-call | tf_op jit(solution)/shard_map/exchange/pallas_call | solution.py:259
  40.8 5.7 %finish.1 = (f32[2,2,24,768]{3,2,1,0:T(8,128)}, f32[2,2,24,768]{3,2,1,0:T(8,128)}, f32[2,2,24,768]{3,2,1,0:T(8,128)}, bf16[2,2,2,4,4,3,8,768]{7,6,5,4,3,2,1,0:T(...) custom-call(bf16[2,2,2,4,4,3,8,768]{7,6,5,4,3,2,1,0:T(8,128)(2,1)S(1)} %get-tuple-element.19.gathered, ...), custom_call_target="tpu_custom_call" | custom-call | tf_op jit(solution)/shard_map/finish/pallas_call | solution.py:296
Async XLA Ops:
  0.6 2.3 %copy-start.4 = (f32[768,64]{0,1:T(8,128)S(1)}, f32[768,64]{0,1:T(8,128)}, u32[]{:S(2)}) copy-start(f32[768,64]{0,1:T(8,128)} %param.13) | copy-start | bytes 589828
  0.6 2.9 %copy-start = (f32[1004,768]{1,0:T(8,128)S(1)}, f32[1004,768]{1,0:T(8,128)}, u32[]{:S(2)}) copy-start(f32[1004,768]{1,0:T(8,128)} %ge.1) | copy-start | bytes 9252868
  0.7 2.9 %copy-start.3 = (f32[4,24,768]{2,1,0:T(8,128)S(1)}, f32[4,24,768]{2,1,0:T(8,128)}, u32[]{:S(2)}) copy-start(f32[4,24,768]{2,1,0:T(8,128)} %param.9) | copy-start | bytes 884740
  0.7 3.0 %copy-start.2 = (f32[4,24,768]{2,1,0:T(8,128)S(1)}, f32[4,24,768]{2,1,0:T(8,128)}, u32[]{:S(2)}) copy-start(f32[4,24,768]{2,1,0:T(8,128)} %param.8) | copy-start | bytes 884740
  0.7 3.1 %copy-start.5 = (f32[1,4,24,768]{3,2,1,0:T(8,128)S(1)}, f32[1,4,24,768]{3,2,1,0:T(8,128)}, u32[]{:S(2)}) copy-start(f32[1,4,24,768]{3,2,1,0:T(8,128)} %param.7) | copy-start | bytes 884740
  3.7 1.9 %copy-start.1 = (f32[1004,768]{1,0:T(8,128)S(1)}, f32[1004,768]{1,0:T(8,128)}, u32[]{:S(2)}) copy-start(f32[1004,768]{1,0:T(8,128)} %me.1) | copy-start | bytes 9252868

commit v2 on v1

--- a/solution.py
+++ b/solution.py
@@ -10,7 +10,7 @@
 OUTER_MOMENTUM = 0.9
 OUTER_RATE = 0.7
 MESH = pl.DeviceIdType.MESH
-HBM = pl.BlockSpec(memory_space=pl.ANY)
+HBM = pl.BlockSpec(memory_space=pltpu.HBM)
 VMEM = pl.BlockSpec(memory_space=pltpu.VMEM)
 X, Y, Z = 0, 1, 2
 ORDERS = ((X, Y, Z), (Y, Z, X), (Z, X, Y))
@@ -48,8 +48,8 @@
 
 def exchange_kernel(
     ll, gl, ml, le, ge, me, bt,
-    gathered, ge_v, me_v, low_total, layer_total,
-    ll_v, gl_v, ml_v, ll_other, part_sum, part_other, le_v, bt_v, low, low_in, low_half, low_other,
+    gathered, ge_v, me_v, low_total, layer_total, bt_v, gl_v, ml_v,
+    ll_v, ll_other, part_sum, part_other, le_v, low, low_in, low_half, low_other,
     load_sem, rep_send, rep_recv, ring_send, ring_recv, pair_send, pair_recv,
 ):
     at, core = where_am_i()
@@ -57,7 +57,7 @@
     z_low = lax.rem(at[Z], 2)
     twin_at = [at[X], at[Y], at[Z] + 1 - 2 * z_low]
     pair, twin = device(at, other), device(twin_at, core)
-    rows = le.shape[0]
+    rows = ge.shape[0]
 
     def remote(src, dst, sems, i, to):
         send, recv = sems
@@ -65,8 +65,8 @@
 
     loads = [
         pltpu.make_async_copy(ll.at[:, core], ll_v, load_sem.at[0]),
-        pltpu.make_async_copy(gl.at[:, core], gl_v, load_sem.at[1]),
-        pltpu.make_async_copy(ml.at[z_low, core], ml_v, load_sem.at[2]),
+        pltpu.make_async_copy(gl, gl_v, load_sem.at[1]),
+        pltpu.make_async_copy(ml, ml_v, load_sem.at[2]),
         pltpu.make_async_copy(bt, bt_v, load_sem.at[3]),
         pltpu.make_async_copy(le, le_v, load_sem.at[4]),
         pltpu.make_async_copy(ge, ge_v, load_sem.at[5]),
@@ -87,7 +87,8 @@
     loads[0].wait()
     loads[1].wait()
     to_pair.wait_recv()
-    part_sum[...] = (gl_v[...] - ll_v[...]) + (gl_v[...] - ll_other[...])
+    weights = gl_v[:, core]
+    part_sum[...] = ((weights - ll_v[...]) + (weights - ll_other[...])).astype(jnp.bfloat16)
     first = remote(part_sum.at[1 - z_low], part_other.at[1 - z_low], rep, 1, twin)
     second = remote(part_sum.at[z_low], part_other.at[z_low], rep, 2, twin)
     first.start()
@@ -100,11 +101,15 @@
     none = jnp.zeros_like(basis)
     left, right = jnp.concatenate([basis, none], 0), jnp.concatenate([none, basis], 0)
     nt = (((1,), (1,)), ((), ()))
+
+    def local_rows(start, size):
+        return jnp.concatenate([le_v[pl.ds(6 * start + c, size, 6), :] for c in range(6)], 1)
+
     for start in range(0, HALF, 128):
         tail = min(128, rows - HALF - start)
         a, b = pl.ds(start, 128), pl.ds(HALF + start, tail)
-        da = (ge_v[a, :] - le_v[a, :]).astype(jnp.bfloat16)
-        db = (ge_v[b, :] - le_v[b, :]).astype(jnp.bfloat16)
+        da = (ge_v[a, :] - local_rows(start, 128)).astype(jnp.bfloat16)
+        db = (ge_v[b, :] - local_rows(HALF + start, tail)).astype(jnp.bfloat16)
         pa = lax.dot_general(da, left, nt, preferred_element_type=jnp.float32)
         pb = lax.dot_general(db, right, nt, preferred_element_type=jnp.float32)
         low[a, :] = pa
@@ -117,8 +122,8 @@
     loads[2].wait()
     first_in = remote(part_sum.at[z_low], part_other.at[z_low], rep, 1, twin)
     first_in.wait_recv()
-    mean = (part_sum[z_low] + part_other[z_low]) / 4
-    _, weights = outer_update(mean, ml_v[...], gl_v[z_low])
+    mean = (part_sum[z_low].astype(jnp.float32) + part_other[z_low].astype(jnp.float32)) / 4
+    _, weights = outer_update(mean, ml_v[z_low, core], gl_v[z_low, core])
     gathered[z_low, core, lax.div(at[Z], 2), at[X], at[Y]] = weights.astype(jnp.bfloat16).reshape(3, 8, 768)
 
     ring, pairs = (ring_send, ring_recv), (pair_send, pair_recv)
@@ -173,7 +178,7 @@
 
     second_in = remote(part_sum.at[1 - z_low], part_other.at[1 - z_low], rep, 2, twin)
     second_in.wait_recv()
-    layer_total[:, core] = part_sum[...] + part_other[...]
+    layer_total[:, core] = part_sum[...].astype(jnp.float32) + part_other[...].astype(jnp.float32)
     total_back = remote(layer_total.at[:, core], layer_total.at[:, core], rep, 6, pair)
     total_back.start()
 
@@ -256,7 +261,7 @@
     bt = proj_basis.T
     f32, bf16 = jnp.float32, jnp.bfloat16
     dma = pltpu.SemaphoreType.DMA
-    gathered, ge_v, me_v, low_total, layer_total = pl.pallas_call(
+    kept = pl.pallas_call(
         exchange_kernel,
         out_shape=(
             pltpu.VMEM((2, 2, 2, 4, 4, 3, 8, 768), bf16),
@@ -264,18 +269,18 @@
             pltpu.VMEM((rows, 768), f32),
             pltpu.VMEM((HALF, 128), f32),
             pltpu.VMEM(grouped, f32),
+            pltpu.VMEM((64, 768), f32),
+            pltpu.VMEM(grouped, f32),
+            pltpu.VMEM(grouped, f32),
         ),
         in_specs=[HBM] * 7,
-        out_specs=(VMEM,) * 5,
+        out_specs=(VMEM,) * 8,
         scratch_shapes=[
             pltpu.VMEM((2, 24, 768), f32),
             pltpu.VMEM((2, 24, 768), f32),
-            pltpu.VMEM((24, 768), f32),
-            pltpu.VMEM((2, 24, 768), f32),
-            pltpu.VMEM((2, 24, 768), f32),
-            pltpu.VMEM((2, 24, 768), f32),
-            pltpu.VMEM((rows, 768), f32),
-            pltpu.VMEM((64, 768), f32),
+            pltpu.VMEM((2, 24, 768), bf16),
+            pltpu.VMEM((2, 24, 768), bf16),
+            pltpu.VMEM((rows * 6, 128), f32),
             pltpu.VMEM((HALF, 128), f32),
             pltpu.VMEM((HALF // 2, 128), f32),
             pltpu.VMEM((HALF // 2, 128), bf16),
@@ -289,10 +294,10 @@
             dma((57,)),
         ],
         compiler_params=pltpu.CompilerParams(
-            collective_id=0, has_side_effects=True, vmem_limit_bytes=24 << 20
+            collective_id=0, has_side_effects=True, vmem_limit_bytes=52 << 20
         ),
         name="exchange",
-    )(ll, gl, ml, local_embed.reshape(rows, 768), global_embed, momentum_embed, bt)
+    )(ll, gl, ml, local_embed.reshape(rows * 6, 128), global_embed, momentum_embed, bt)
     outs = pl.pallas_call(
         finish_kernel,
         out_shape=(
@@ -305,7 +310,7 @@
         scratch_shapes=[pltpu.VMEM(grouped, f32)] * 3 + [pltpu.VMEM((rows, 768), f32)] * 3 + [dma((4,)), dma((24,))],
         compiler_params=pltpu.CompilerParams(vmem_limit_bytes=24 << 20),
         name="finish",
-    )(gathered, ge_v, me_v, low_total, layer_total, bt, gl, ml)
+    )(*kept)
     layers = [a.reshape(4, 24, 768) for a in outs[:3]]
     return (*layers, outs[3].reshape(4, 768, 768), *outs[4:])
 

time: 46.7 us -> 39.2 us (0.84)
  local copies, waits for them, and re-layouts: 4.93 us -> 0 us
  Pallas kernels: 40.9 us -> 38.5 us
    unnamed x13 -> x0, local copies, waits for them, and re-layouts: 4.93 us -> none
    pallas_call x1, Pallas kernels: 35.2 us -> 32.7 us  [body(): pl.pallas_call(exchange_kernel, out_shape=(pltpu.VMEM((2, 2, 2, 4, 4, 3,...]
where the time goes in v2:
time: 39.2 us; the launch traced here: 39.1 us
  Pallas kernels  38.5 us (98%)
  between operations  0.64 us (2%)
    pallas_call x1, Pallas kernels, body(): pl.pallas_call(exchange_kernel, out_shape=(pltpu.VMEM((2, 2, 2, 4, 4, 3,...  32.7 us
    pallas_call x1, Pallas kernels, body(): pl.pallas_call(finish_kernel, out_shape=(*[jax.ShapeDtypeStruct(grouped,...  5.74 us

profile of v2, /device:TPU:1, one launch (start us, length us, event | category | flops | bytes accessed | tf_op | source)
XLA Modules:
  0.0 39.1 jit_solution(14914284740777214309)
XLA Ops:
  0.6 32.7 %exchange.1 = (bf16[2,2,2,4,4,3,8,768]{7,6,5,4,3,2,1,0:T(8,128)(2,1)S(1)}, f32[1004,768]{1,0:T(8,128)S(1)}, f32[1004,768]{1,0:T(8,128)S(1)}, f32[512,128]{1,0:T(...) custom-call(f32[2,2,24,768]{3,2,1,0:T(8,128)} %bitcast.10, ...), custom_call_target="tpu_custom_call" | custom-call | tf_op jit(solution)/shard_map/exchange/pallas_call | solution.py:264
  33.4 5.7 %finish.1 = (f32[2,2,24,768]{3,2,1,0:T(8,128)}, f32[2,2,24,768]{3,2,1,0:T(8,128)}, f32[2,2,24,768]{3,2,1,0:T(8,128)}, bf16[2,2,2,4,4,3,8,768]{7,6,5,4,3,2,1,0:T(...) custom-call(bf16[2,2,2,4,4,3,8,768]{7,6,5,4,3,2,1,0:T(8,128)(2,1)S(1)} %get-tuple-element.22.gathered, ...), custom_call_target="tpu_custom_call" | custom-call | tf_op jit(solution)/shard_map/finish/pallas_call | solution.py:301

commit v3 on v2

--- a/solution.py
+++ b/solution.py
@@ -72,7 +72,7 @@
         pltpu.make_async_copy(ge, ge_v, load_sem.at[5]),
         pltpu.make_async_copy(me, me_v, load_sem.at[6]),
     ]
-    for load in loads:
+    for load in loads[:6]:
         load.start()
 
     barrier = pltpu.get_barrier_semaphore()
@@ -97,6 +97,7 @@
     loads[3].wait()
     loads[4].wait()
     loads[5].wait()
+    loads[6].start()
     basis = bt_v[...].astype(jnp.bfloat16)
     none = jnp.zeros_like(basis)
     left, right = jnp.concatenate([basis, none], 0), jnp.concatenate([none, basis], 0)
@@ -130,14 +131,13 @@
     started, expected = [], []
 
     def send(where, part, slot, to):
-        copy = remote(piece(gathered, where, core, part), piece(gathered, where, core, part), ring, part * 18 + slot, to)
+        copy = remote(piece(gathered, where, core, part), piece(gathered, where, core, part), ring, part * 27 + slot, to)
         copy.start()
         started.append(copy)
 
     def arrive(where, part, slot):
         ref = piece(gathered, where, core, part)
-        remote(ref, ref, ring, part * 18 + slot, pair).wait_recv()
-        share(where, part, slot)
+        remote(ref, ref, ring, part * 27 + slot, pair).wait_recv()
 
     def share(where, part, slot):
         ref = piece(gathered, where, core, part)
@@ -153,6 +153,9 @@
     for part, (d1, d2, d3) in enumerate(ORDERS):
         for i, step in enumerate(DELTAS):
             send(at, part, i, device(moved(at, d1, step), core))
+    for part, (d1, d2, d3) in enumerate(ORDERS):
+        for j, step in enumerate(DELTAS):
+            send(at, part, 3 + 4 * j, device(moved(at, d2, step), core))
     for part in range(3):
         share(at, part, 18)
 
@@ -162,14 +165,26 @@
     low_to_twin = remote(low_half, low_other, rep, 4, twin)
     low_to_twin.start()
 
+    for i, back in enumerate(DELTAS):
+        for part, (d1, d2, d3) in enumerate(ORDERS):
+            chunk = moved(at, d1, 4 - back)
+            arrive(chunk, part, i)
+            for j, step in enumerate(DELTAS):
+                send(chunk, part, 4 + 4 * j + i, device(moved(at, d2, step), core))
+            share(chunk, part, i)
     for part, (d1, d2, d3) in enumerate(ORDERS):
-        for i, step in enumerate(DELTAS):
-            arrive(moved(at, d1, 4 - step), part, i)
-        row = opened(at, d1)
-        for i, step in enumerate(DELTAS):
-            send(row, part, 3 + i, device(moved(at, d2, step), core))
         for i, step in enumerate((1, 3)):
-            send(row, part, 6 + i, device(moved(at, d3, step), core))
+            send(opened(at, d1), part, 15 + i, device(moved(at, d3, step), core))
+
+    for j, back in enumerate(DELTAS):
+        for part, (d1, d2, d3) in enumerate(ORDERS):
+            first_chunk = moved(at, d2, 4 - back)
+            for k, across in enumerate((0,) + DELTAS):
+                arrive(moved(first_chunk, d1, 4 - across), part, 3 + 4 * j + k)
+            row = opened(first_chunk, d1)
+            for i, step in enumerate((1, 3)):
+                send(row, part, 17 + 2 * j + i, device(moved(at, d3, step), core))
+            share(row, part, 3 + j)
 
     low_to_twin.wait_recv()
     low_total[mine, :] = low_half[...].astype(jnp.float32) + low_other[...].astype(jnp.float32)
@@ -182,23 +197,19 @@
     total_back = remote(layer_total.at[:, core], layer_total.at[:, core], rep, 6, pair)
     total_back.start()
 
-    for j, back in enumerate(DELTAS):
-        for part, (d1, d2, d3) in enumerate(ORDERS):
-            row = opened(moved(at, d2, 4 - back), d1)
-            arrive(row, part, 3 + j)
-            for i, step in enumerate((1, 3)):
-                send(row, part, 8 + 2 * j + i, device(moved(at, d3, step), core))
-
     for j, back in enumerate((0,) + DELTAS):
         for part, (d1, d2, d3) in enumerate(ORDERS):
             for i, step in enumerate((1, 3)):
                 row = opened(moved(moved(at, d2, 4 - back), d3, 4 - step), d1)
-                arrive(row, part, 6 + 2 * j + i)
+                arrive(row, part, 15 + 2 * j + i)
                 if j // 2 == i:
-                    send(row, part, 14 + j, device(moved(at, d3, step), core))
+                    send(row, part, 23 + j, device(moved(at, d3, step), core))
+                share(row, part, 6 + 2 * j + i)
     for j, back in enumerate((0,) + DELTAS):
         for part, (d1, d2, d3) in enumerate(ORDERS):
-            arrive(opened(moved(moved(at, d2, 4 - back), d3, 2), d1), part, 14 + j)
+            row = opened(moved(moved(at, d2, 4 - back), d3, 2), d1)
+            arrive(row, part, 23 + j)
+            share(row, part, 14 + j)
 
     remote(low_total.at[theirs], low_total.at[theirs], rep, 5, pair).wait_recv()
     remote(layer_total.at[:, other], layer_total.at[:, other], rep, 6, pair).wait_recv()
@@ -288,8 +299,8 @@
             dma((7,)),
             dma((7,)),
             dma((7,)),
-            dma((54,)),
-            dma((54,)),
+            dma((81,)),
+            dma((81,)),
             dma((57,)),
             dma((57,)),
         ],

time: 39.2 us -> 38.5 us (0.982)
  Pallas kernels: 38.5 us -> 37.8 us
    pallas_call x1, Pallas kernels: 32.7 us -> 32 us  [body(): pl.pallas_call(exchange_kernel, out_shape=(pltpu.VMEM((2, 2, 2, 4, 4, 3,...]
where the time goes in v3:
time: 38.5 us; the launch traced here: 38.4 us
  Pallas kernels  37.8 us (98%)
  between operations  0.64 us (2%)
    pallas_call x1, Pallas kernels, body(): pl.pallas_call(exchange_kernel, out_shape=(pltpu.VMEM((2, 2, 2, 4, 4, 3,...  32 us
    pallas_call x1, Pallas kernels, body(): pl.pallas_call(finish_kernel, out_shape=(*[jax.ShapeDtypeStruct(grouped,...  5.74 us

profile of v3, /device:TPU:1, one launch (start us, length us, event | category | flops | bytes accessed | tf_op | source)
XLA Modules:
  0.0 38.4 jit_solution(11220896142161465927)
XLA Ops:
  0.6 32.0 %exchange.1 = (bf16[2,2,2,4,4,3,8,768]{7,6,5,4,3,2,1,0:T(8,128)(2,1)S(1)}, f32[1004,768]{1,0:T(8,128)S(1)}, f32[1004,768]{1,0:T(8,128)S(1)}, f32[512,128]{1,0:T(...) custom-call(f32[2,2,24,768]{3,2,1,0:T(8,128)} %bitcast.10, ...), custom_call_target="tpu_custom_call" | custom-call | tf_op jit(solution)/shard_map/exchange/pallas_call | solution.py:275
  32.7 5.7 %finish.1 = (f32[2,2,24,768]{3,2,1,0:T(8,128)}, f32[2,2,24,768]{3,2,1,0:T(8,128)}, f32[2,2,24,768]{3,2,1,0:T(8,128)}, bf16[2,2,2,4,4,3,8,768]{7,6,5,4,3,2,1,0:T(...) custom-call(bf16[2,2,2,4,4,3,8,768]{7,6,5,4,3,2,1,0:T(8,128)(2,1)S(1)} %get-tuple-element.22.gathered, ...), custom_call_target="tpu_custom_call" | custom-call | tf_op jit(solution)/shard_map/finish/pallas_call | solution.py:312

commit v4 on v3

--- a/solution.py
+++ b/solution.py
@@ -64,7 +64,7 @@
         return pltpu.make_async_remote_copy(src, dst, send.at[i], recv.at[i], device_id=to, device_id_type=MESH)
 
     loads = [
-        pltpu.make_async_copy(ll.at[:, core], ll_v, load_sem.at[0]),
+        pltpu.make_async_copy(ll, ll_v, load_sem.at[0]),
         pltpu.make_async_copy(gl, gl_v, load_sem.at[1]),
         pltpu.make_async_copy(ml, ml_v, load_sem.at[2]),
         pltpu.make_async_copy(bt, bt_v, load_sem.at[3]),
@@ -72,23 +72,25 @@
         pltpu.make_async_copy(ge, ge_v, load_sem.at[5]),
         pltpu.make_async_copy(me, me_v, load_sem.at[6]),
     ]
-    for load in loads[:6]:
+    for load in loads[:4]:
         load.start()
 
     barrier = pltpu.get_barrier_semaphore()
     peers = [pair] + [device(moved(at, axis, step), core) for axis in (X, Y, Z) for step in DELTAS]
     for peer in peers:
         pl.semaphore_signal(barrier, inc=1, device_id=peer, device_id_type=MESH)
+    loads[0].wait()
+    loads[4].start()
+    loads[5].start()
     pl.semaphore_wait(barrier, len(peers))
 
     rep = (rep_send, rep_recv)
-    to_pair = remote(ll.at[:, other], ll_other, rep, 0, pair)
+    to_pair = remote(ll_v.at[:, other], ll_other, rep, 0, pair)
     to_pair.start()
-    loads[0].wait()
     loads[1].wait()
     to_pair.wait_recv()
     weights = gl_v[:, core]
-    part_sum[...] = ((weights - ll_v[...]) + (weights - ll_other[...])).astype(jnp.bfloat16)
+    part_sum[...] = ((weights - ll_v[:, core]) + (weights - ll_other[...])).astype(jnp.bfloat16)
     first = remote(part_sum.at[1 - z_low], part_other.at[1 - z_low], rep, 1, twin)
     second = remote(part_sum.at[z_low], part_other.at[z_low], rep, 2, twin)
     first.start()
@@ -106,7 +108,7 @@
     def local_rows(start, size):
         return jnp.concatenate([le_v[pl.ds(6 * start + c, size, 6), :] for c in range(6)], 1)
 
-    for start in range(0, HALF, 128):
+    def low_rank(start):
         tail = min(128, rows - HALF - start)
         a, b = pl.ds(start, 128), pl.ds(HALF + start, tail)
         da = (ge_v[a, :] - local_rows(start, 128)).astype(jnp.bfloat16)
@@ -115,10 +117,8 @@
         pb = lax.dot_general(db, right, nt, preferred_element_type=jnp.float32)
         low[a, :] = pa
         low[pl.ds(start, tail), :] = low[pl.ds(start, tail), :] + pb
-    quarter = HALF // 2
-    mine, theirs = pl.ds(core * quarter, quarter), pl.ds(other * quarter, quarter)
-    low_to_pair = remote(low.at[theirs], low_in, rep, 3, pair)
-    low_to_pair.start()
+    for start in range(0, HALF // 2, 128):
+        low_rank(start)
 
     loads[2].wait()
     first_in = remote(part_sum.at[z_low], part_other.at[z_low], rep, 1, twin)
@@ -154,11 +154,17 @@
         for i, step in enumerate(DELTAS):
             send(at, part, i, device(moved(at, d1, step), core))
     for part, (d1, d2, d3) in enumerate(ORDERS):
-        for j, step in enumerate(DELTAS):
+        for j, step in enumerate((1, 3)):
             send(at, part, 3 + 4 * j, device(moved(at, d2, step), core))
     for part in range(3):
         share(at, part, 18)
 
+    for start in range(HALF // 2, HALF, 128):
+        low_rank(start)
+    quarter = HALF // 2
+    mine, theirs = pl.ds(core * quarter, quarter), pl.ds(other * quarter, quarter)
+    low_to_pair = remote(low.at[theirs], low_in, rep, 3, pair)
+    low_to_pair.start()
     low_to_pair.wait_recv()
     half = low[mine, :] + low_in[...]
     low_half[...] = half.astype(jnp.bfloat16)
@@ -169,7 +175,7 @@
         for part, (d1, d2, d3) in enumerate(ORDERS):
             chunk = moved(at, d1, 4 - back)
             arrive(chunk, part, i)
-            for j, step in enumerate(DELTAS):
+            for j, step in enumerate((1, 3)):
                 send(chunk, part, 4 + 4 * j + i, device(moved(at, d2, step), core))
             share(chunk, part, i)
     for part, (d1, d2, d3) in enumerate(ORDERS):
@@ -180,7 +186,10 @@
         for part, (d1, d2, d3) in enumerate(ORDERS):
             first_chunk = moved(at, d2, 4 - back)
             for k, across in enumerate((0,) + DELTAS):
-                arrive(moved(first_chunk, d1, 4 - across), part, 3 + 4 * j + k)
+                chunk = moved(first_chunk, d1, 4 - across)
+                arrive(chunk, part, 3 + 4 * j + k)
+                if j == k // 2:
+                    send(chunk, part, 11 + k, device(moved(at, d2, back), core))
             row = opened(first_chunk, d1)
             for i, step in enumerate((1, 3)):
                 send(row, part, 17 + 2 * j + i, device(moved(at, d3, step), core))
@@ -287,7 +296,7 @@
         in_specs=[HBM] * 7,
         out_specs=(VMEM,) * 8,
         scratch_shapes=[
-            pltpu.VMEM((2, 24, 768), f32),
+            pltpu.VMEM(grouped, f32),
             pltpu.VMEM((2, 24, 768), f32),
             pltpu.VMEM((2, 24, 768), bf16),
             pltpu.VMEM((2, 24, 768), bf16),

time: 38.5 us -> 39.8 us (1.034)
  Pallas kernels: 37.8 us -> 39 us
    pallas_call x1, Pallas kernels: 32 us -> 33.3 us  [body(): pl.pallas_call(exchange_kernel, out_shape=(pltpu.VMEM((2, 2, 2, 4, 4, 3,...]
where the time goes in v4:
time: 39.8 us; the launch traced here: 39.6 us
  Pallas kernels  39 us (98%)
  between operations  0.64 us (2%)
    pallas_call x1, Pallas kernels, body(): pl.pallas_call(exchange_kernel, out_shape=(pltpu.VMEM((2, 2, 2, 4, 4, 3,...  33.3 us
    pallas_call x1, Pallas kernels, body(): pl.pallas_call(finish_kernel, out_shape=(*[jax.ShapeDtypeStruct(grouped,...  5.74 us

profile of v4, /device:TPU:1, one launch (start us, length us, event | category | flops | bytes accessed | tf_op | source)
XLA Modules:
  0.0 39.6 jit_solution(8526792335495225676)
XLA Ops:
  0.6 33.3 %exchange.1 = (bf16[2,2,2,4,4,3,8,768]{7,6,5,4,3,2,1,0:T(8,128)(2,1)S(1)}, f32[1004,768]{1,0:T(8,128)S(1)}, f32[1004,768]{1,0:T(8,128)S(1)}, f32[512,128]{1,0:T(...) custom-call(f32[2,2,24,768]{3,2,1,0:T(8,128)} %bitcast.10, ...), custom_call_target="tpu_custom_call" | custom-call | tf_op jit(solution)/shard_map/exchange/pallas_call | solution.py:284
  33.9 5.7 %finish.1 = (f32[2,2,24,768]{3,2,1,0:T(8,128)}, f32[2,2,24,768]{3,2,1,0:T(8,128)}, f32[2,2,24,768]{3,2,1,0:T(8,128)}, bf16[2,2,2,4,4,3,8,768]{7,6,5,4,3,2,1,0:T(...) custom-call(bf16[2,2,2,4,4,3,8,768]{7,6,5,4,3,2,1,0:T(8,128)(2,1)S(1)} %get-tuple-element.22.gathered, ...), custom_call_target="tpu_custom_call" | custom-call | tf_op jit(solution)/shard_map/finish/pallas_call | solution.py:321

commit v5 on v3

--- a/solution.py
+++ b/solution.py
@@ -154,10 +154,21 @@
         for i, step in enumerate(DELTAS):
             send(at, part, i, device(moved(at, d1, step), core))
     for part, (d1, d2, d3) in enumerate(ORDERS):
-        for j, step in enumerate(DELTAS):
+        for j, step in enumerate((1, 3)):
             send(at, part, 3 + 4 * j, device(moved(at, d2, step), core))
     for part in range(3):
         share(at, part, 18)
+
+    for i, back in enumerate(DELTAS):
+        for part, (d1, d2, d3) in enumerate(ORDERS):
+            chunk = moved(at, d1, 4 - back)
+            arrive(chunk, part, i)
+            for j, step in enumerate((1, 3)):
+                send(chunk, part, 4 + 4 * j + i, device(moved(at, d2, step), core))
+            share(chunk, part, i)
+    for part, (d1, d2, d3) in enumerate(ORDERS):
+        for i, step in enumerate((1, 3)):
+            send(opened(at, d1), part, 15 + i, device(moved(at, d3, step), core))
 
     low_to_pair.wait_recv()
     half = low[mine, :] + low_in[...]
@@ -165,22 +176,14 @@
     low_to_twin = remote(low_half, low_other, rep, 4, twin)
     low_to_twin.start()
 
-    for i, back in enumerate(DELTAS):
-        for part, (d1, d2, d3) in enumerate(ORDERS):
-            chunk = moved(at, d1, 4 - back)
-            arrive(chunk, part, i)
-            for j, step in enumerate(DELTAS):
-                send(chunk, part, 4 + 4 * j + i, device(moved(at, d2, step), core))
-            share(chunk, part, i)
-    for part, (d1, d2, d3) in enumerate(ORDERS):
-        for i, step in enumerate((1, 3)):
-            send(opened(at, d1), part, 15 + i, device(moved(at, d3, step), core))
-
     for j, back in enumerate(DELTAS):
         for part, (d1, d2, d3) in enumerate(ORDERS):
             first_chunk = moved(at, d2, 4 - back)
             for k, across in enumerate((0,) + DELTAS):
-                arrive(moved(first_chunk, d1, 4 - across), part, 3 + 4 * j + k)
+                chunk = moved(first_chunk, d1, 4 - across)
+                arrive(chunk, part, 3 + 4 * j + k)
+                if j == k // 2:
+                    send(chunk, part, 11 + k, device(moved(at, d2, back), core))
             row = opened(first_chunk, d1)
             for i, step in enumerate((1, 3)):
                 send(row, part, 17 + 2 * j + i, device(moved(at, d3, step), core))

time: 38.5 us -> 40.3 us (1.047)
  Pallas kernels: 37.8 us -> 39.5 us
    pallas_call x1, Pallas kernels: 32 us -> 33.8 us  [body(): pl.pallas_call(exchange_kernel, out_shape=(pltpu.VMEM((2, 2, 2, 4, 4, 3,...]
where the time goes in v5:
time: 40.3 us; the launch traced here: 40.1 us
  Pallas kernels  39.5 us (98%)
  between operations  0.64 us (2%)
    pallas_call x1, Pallas kernels, body(): pl.pallas_call(exchange_kernel, out_shape=(pltpu.VMEM((2, 2, 2, 4, 4, 3,...  33.8 us
    pallas_call x1, Pallas kernels, body(): pl.pallas_call(finish_kernel, out_shape=(*[jax.ShapeDtypeStruct(grouped,...  5.74 us

profile of v5, /device:TPU:1, one launch (start us, length us, event | category | flops | bytes accessed | tf_op | source)
XLA Modules:
  0.0 40.1 jit_solution(3834307156037605071)
XLA Ops:
  0.6 33.8 %exchange.1 = (bf16[2,2,2,4,4,3,8,768]{7,6,5,4,3,2,1,0:T(8,128)(2,1)S(1)}, f32[1004,768]{1,0:T(8,128)S(1)}, f32[1004,768]{1,0:T(8,128)S(1)}, f32[512,128]{1,0:T(...) custom-call(f32[2,2,24,768]{3,2,1,0:T(8,128)} %bitcast.10, ...), custom_call_target="tpu_custom_call" | custom-call | tf_op jit(solution)/shard_map/exchange/pallas_call | solution.py:278
  34.4 5.7 %finish.1 = (f32[2,2,24,768]{3,2,1,0:T(8,128)}, f32[2,2,24,768]{3,2,1,0:T(8,128)}, f32[2,2,24,768]{3,2,1,0:T(8,128)}, bf16[2,2,2,4,4,3,8,768]{7,6,5,4,3,2,1,0:T(...) custom-call(bf16[2,2,2,4,4,3,8,768]{7,6,5,4,3,2,1,0:T(8,128)(2,1)S(1)} %get-tuple-element.22.gathered, ...), custom_call_target="tpu_custom_call" | custom-call | tf_op jit(solution)/shard_map/finish/pallas_call | solution.py:315

commit v6 on v3

--- a/solution.py
+++ b/solution.py
@@ -153,9 +153,6 @@
     for part, (d1, d2, d3) in enumerate(ORDERS):
         for i, step in enumerate(DELTAS):
             send(at, part, i, device(moved(at, d1, step), core))
-    for part, (d1, d2, d3) in enumerate(ORDERS):
-        for j, step in enumerate(DELTAS):
-            send(at, part, 3 + 4 * j, device(moved(at, d2, step), core))
     for part in range(3):
         share(at, part, 18)
 
@@ -165,23 +162,22 @@
     low_to_twin = remote(low_half, low_other, rep, 4, twin)
     low_to_twin.start()
 
-    for i, back in enumerate(DELTAS):
-        for part, (d1, d2, d3) in enumerate(ORDERS):
-            chunk = moved(at, d1, 4 - back)
+    for part, (d1, d2, d3) in enumerate(ORDERS):
+        chunks = [moved(at, d1, 4 - back) for back in DELTAS]
+        for i, chunk in enumerate(chunks):
             arrive(chunk, part, i)
-            for j, step in enumerate(DELTAS):
-                send(chunk, part, 4 + 4 * j + i, device(moved(at, d2, step), core))
+        row = opened(at, d1)
+        for j, step in enumerate(DELTAS):
+            send(row, part, 3 + j, device(moved(at, d2, step), core))
+        for i, step in enumerate((1, 3)):
+            send(row, part, 15 + i, device(moved(at, d3, step), core))
+        for i, chunk in enumerate(chunks):
             share(chunk, part, i)
-    for part, (d1, d2, d3) in enumerate(ORDERS):
-        for i, step in enumerate((1, 3)):
-            send(opened(at, d1), part, 15 + i, device(moved(at, d3, step), core))
 
     for j, back in enumerate(DELTAS):
         for part, (d1, d2, d3) in enumerate(ORDERS):
-            first_chunk = moved(at, d2, 4 - back)
-            for k, across in enumerate((0,) + DELTAS):
-                arrive(moved(first_chunk, d1, 4 - across), part, 3 + 4 * j + k)
-            row = opened(first_chunk, d1)
+            row = opened(moved(at, d2, 4 - back), d1)
+            arrive(row, part, 3 + j)
             for i, step in enumerate((1, 3)):
                 send(row, part, 17 + 2 * j + i, device(moved(at, d3, step), core))
             share(row, part, 3 + j)

time: 38.5 us -> 39.7 us (1.031)
  Pallas kernels: 37.8 us -> 38.9 us
    pallas_call x1, Pallas kernels: 32 us -> 33.2 us  [body(): pl.pallas_call(exchange_kernel, out_shape=(pltpu.VMEM((2, 2, 2, 4, 4, 3,...]
where the time goes in v6:
time: 39.7 us; the launch traced here: 39.6 us
  Pallas kernels  38.9 us (98%)
  between operations  0.64 us (2%)
    pallas_call x1, Pallas kernels, body(): pl.pallas_call(exchange_kernel, out_shape=(pltpu.VMEM((2, 2, 2, 4, 4, 3,...  33.2 us
    pallas_call x1, Pallas kernels, body(): pl.pallas_call(finish_kernel, out_shape=(*[jax.ShapeDtypeStruct(grouped,...  5.74 us

profile of v6, /device:TPU:1, one launch (start us, length us, event | category | flops | bytes accessed | tf_op | source)
XLA Modules:
  0.0 39.6 jit_solution(11462695248980773094)
XLA Ops:
  0.6 33.2 %exchange.1 = (bf16[2,2,2,4,4,3,8,768]{7,6,5,4,3,2,1,0:T(8,128)(2,1)S(1)}, f32[1004,768]{1,0:T(8,128)S(1)}, f32[1004,768]{1,0:T(8,128)S(1)}, f32[512,128]{1,0:T(...) custom-call(f32[2,2,24,768]{3,2,1,0:T(8,128)} %bitcast.10, ...), custom_call_target="tpu_custom_call" | custom-call | tf_op jit(solution)/shard_map/exchange/pallas_call | solution.py:271
  33.8 5.7 %finish.1 = (f32[2,2,24,768]{3,2,1,0:T(8,128)}, f32[2,2,24,768]{3,2,1,0:T(8,128)}, f32[2,2,24,768]{3,2,1,0:T(8,128)}, bf16[2,2,2,4,4,3,8,768]{7,6,5,4,3,2,1,0:T(...) custom-call(bf16[2,2,2,4,4,3,8,768]{7,6,5,4,3,2,1,0:T(8,128)(2,1)S(1)} %get-tuple-element.22.gathered, ...), custom_call_target="tpu_custom_call" | custom-call | tf_op jit(solution)/shard_map/finish/pallas_call | solution.py:308

commit v7 on v5

--- a/solution.py
+++ b/solution.py
@@ -93,6 +93,45 @@
     second = remote(part_sum.at[z_low], part_other.at[z_low], rep, 2, twin)
     first.start()
     second.start()
+
+    loads[2].wait()
+    first_in = remote(part_sum.at[z_low], part_other.at[z_low], rep, 1, twin)
+    first_in.wait_recv()
+    mean = (part_sum[z_low].astype(jnp.float32) + part_other[z_low].astype(jnp.float32)) / 4
+    _, weights = outer_update(mean, ml_v[z_low, core], gl_v[z_low, core])
+    gathered[z_low, core, lax.div(at[Z], 2), at[X], at[Y]] = weights.astype(jnp.bfloat16).reshape(3, 8, 768)
+
+    ring, pairs = (ring_send, ring_recv), (pair_send, pair_recv)
+    started, expected = [], []
+
+    def send(where, part, slot, to):
+        copy = remote(piece(gathered, where, core, part), piece(gathered, where, core, part), ring, part * 27 + slot, to)
+        copy.start()
+        started.append(copy)
+
+    def arrive(where, part, slot):
+        ref = piece(gathered, where, core, part)
+        remote(ref, ref, ring, part * 27 + slot, pair).wait_recv()
+
+    def share(where, part, slot):
+        ref = piece(gathered, where, core, part)
+        copy = remote(ref, ref, pairs, part * 19 + slot, pair)
+        copy.start()
+        started.append(copy)
+        back = piece(gathered, where, other, part)
+        expected.append(remote(back, back, pairs, part * 19 + slot, pair))
+
+    def opened(where, *axes):
+        return [None if i in axes else c for i, c in enumerate(where)]
+
+    for part, (d1, d2, d3) in enumerate(ORDERS):
+        for i, step in enumerate(DELTAS):
+            send(at, part, i, device(moved(at, d1, step), core))
+    for part, (d1, d2, d3) in enumerate(ORDERS):
+        for j, step in enumerate(DELTAS):
+            send(at, part, 3 + 4 * j, device(moved(at, d2, step), core))
+    for part in range(3):
+        share(at, part, 18)
 
     loads[3].wait()
     loads[4].wait()
@@ -120,50 +159,11 @@
     low_to_pair = remote(low.at[theirs], low_in, rep, 3, pair)
     low_to_pair.start()
 
-    loads[2].wait()
-    first_in = remote(part_sum.at[z_low], part_other.at[z_low], rep, 1, twin)
-    first_in.wait_recv()
-    mean = (part_sum[z_low].astype(jnp.float32) + part_other[z_low].astype(jnp.float32)) / 4
-    _, weights = outer_update(mean, ml_v[z_low, core], gl_v[z_low, core])
-    gathered[z_low, core, lax.div(at[Z], 2), at[X], at[Y]] = weights.astype(jnp.bfloat16).reshape(3, 8, 768)
-
-    ring, pairs = (ring_send, ring_recv), (pair_send, pair_recv)
-    started, expected = [], []
-
-    def send(where, part, slot, to):
-        copy = remote(piece(gathered, where, core, part), piece(gathered, where, core, part), ring, part * 27 + slot, to)
-        copy.start()
-        started.append(copy)
-
-    def arrive(where, part, slot):
-        ref = piece(gathered, where, core, part)
-        remote(ref, ref, ring, part * 27 + slot, pair).wait_recv()
-
-    def share(where, part, slot):
-        ref = piece(gathered, where, core, part)
-        copy = remote(ref, ref, pairs, part * 19 + slot, pair)
-        copy.start()
-        started.append(copy)
-        back = piece(gathered, where, other, part)
-        expected.append(remote(back, back, pairs, part * 19 + slot, pair))
-
-    def opened(where, *axes):
-        return [None if i in axes else c for i, c in enumerate(where)]
-
-    for part, (d1, d2, d3) in enumerate(ORDERS):
-        for i, step in enumerate(DELTAS):
-            send(at, part, i, device(moved(at, d1, step), core))
-    for part, (d1, d2, d3) in enumerate(ORDERS):
-        for j, step in enumerate((1, 3)):
-            send(at, part, 3 + 4 * j, device(moved(at, d2, step), core))
-    for part in range(3):
-        share(at, part, 18)
-
     for i, back in enumerate(DELTAS):
         for part, (d1, d2, d3) in enumerate(ORDERS):
             chunk = moved(at, d1, 4 - back)
             arrive(chunk, part, i)
-            for j, step in enumerate((1, 3)):
+            for j, step in enumerate(DELTAS):
                 send(chunk, part, 4 + 4 * j + i, device(moved(at, d2, step), core))
             share(chunk, part, i)
     for part, (d1, d2, d3) in enumerate(ORDERS):
@@ -180,10 +180,7 @@
         for part, (d1, d2, d3) in enumerate(ORDERS):
             first_chunk = moved(at, d2, 4 - back)
             for k, across in enumerate((0,) + DELTAS):
-                chunk = moved(first_chunk, d1, 4 - across)
-                arrive(chunk, part, 3 + 4 * j + k)
-                if j == k // 2:
-                    send(chunk, part, 11 + k, device(moved(at, d2, back), core))
+                arrive(moved(first_chunk, d1, 4 - across), part, 3 + 4 * j + k)
             row = opened(first_chunk, d1)
             for i, step in enumerate((1, 3)):
                 send(row, part, 17 + 2 * j + i, device(moved(at, d3, step), core))

time: 40.3 us -> 38.5 us (0.955)
  Pallas kernels: 39.5 us -> 37.8 us
    pallas_call x1, Pallas kernels: 33.8 us -> 32 us  [body(): pl.pallas_call(exchange_kernel, out_shape=(pltpu.VMEM((2, 2, 2, 4, 4, 3,...]
where the time goes in v7:
time: 38.5 us; the launch traced here: 38.4 us
  Pallas kernels  37.8 us (98%)
  between operations  0.64 us (2%)
    pallas_call x1, Pallas kernels, body(): pl.pallas_call(exchange_kernel, out_shape=(pltpu.VMEM((2, 2, 2, 4, 4, 3,...  32 us
    pallas_call x1, Pallas kernels, body(): pl.pallas_call(finish_kernel, out_shape=(*[jax.ShapeDtypeStruct(grouped,...  5.74 us

profile of v7, /device:TPU:1, one launch (start us, length us, event | category | flops | bytes accessed | tf_op | source)
XLA Modules:
  0.0 38.4 jit_solution(10021570289173179198)
XLA Ops:
  0.6 32.0 %exchange.1 = (bf16[2,2,2,4,4,3,8,768]{7,6,5,4,3,2,1,0:T(8,128)(2,1)S(1)}, f32[1004,768]{1,0:T(8,128)S(1)}, f32[1004,768]{1,0:T(8,128)S(1)}, f32[512,128]{1,0:T(...) custom-call(f32[2,2,24,768]{3,2,1,0:T(8,128)} %bitcast.10, ...), custom_call_target="tpu_custom_call" | custom-call | tf_op jit(solution)/shard_map/exchange/pallas_call | solution.py:275
  32.7 5.7 %finish.1 = (f32[2,2,24,768]{3,2,1,0:T(8,128)}, f32[2,2,24,768]{3,2,1,0:T(8,128)}, f32[2,2,24,768]{3,2,1,0:T(8,128)}, bf16[2,2,2,4,4,3,8,768]{7,6,5,4,3,2,1,0:T(...) custom-call(bf16[2,2,2,4,4,3,8,768]{7,6,5,4,3,2,1,0:T(8,128)(2,1)S(1)} %get-tuple-element.22.gathered, ...), custom_call_target="tpu_custom_call" | custom-call | tf_op jit(solution)/shard_map/finish/pallas_call | solution.py:312
